TPU v7x, 32 devices: a whole 2x2x4 slice. The times are simulated.
32 devices in a mesh: groups: 2 (over x), ctx: 16 (over z, y, core).
Axes of the slice: x: 2, y: 2, z: 4, core: 2. Of those that a mesh axis runs over, the one named last changes fastest.
Arguments:
- hidden: bfloat16 [4096, 2048], P(('groups', 'ctx')), parts along dimension 0, may hold values from -6 to 6
- w_query: bfloat16 [2048, 2048], P('ctx')
- w_keyval: bfloat16 [2048, 1024], P('ctx')
- w_out: bfloat16 [2048, 2048], P('ctx'), may hold values from -1.796875 to 1.796875
- global_blocks: int32 [4], P('groups'), parts along dimension 0, may hold values from 0 to 15, as said below
- cotangent: bfloat16 [4096, 2048], P(('groups', 'ctx')), parts along dimension 0, may hold values from -6 to 6
Outputs:
- combined: bfloat16 [4096, 2048], P(('groups', 'ctx')), parts along dimension 0
- input_grad: bfloat16 [4096, 2048], P(('groups', 'ctx')), parts along dimension 0
There are 2 independent parts, one for each index of `groups`. A program takes and returns all parts, laid end to end along the dimension named above; an argument that names none is the same for every part. Nothing has to cross between parts.
Inputs may be any that keep to these rules, and one draw needn't show every extreme that they name: `global_blocks`: 2 distinct block indices; the last block, 15, is always one of them, at a position drawn from the seed.
All inputs are finite; a program needn't handle non-finite values.
Results may differ from a plain program's by a relative error of at most 0.0098.
Values may be sent and summed in bfloat16 or wider, within the bound.
No kernel may reach another device: no remote copies, remote signals or barrier semaphores. Data moves between devices by JAX's collectives and lax.ppermute only.
A program may use at most 128 MiB of HBM per device.

v0:
```python
import jax
import jax.numpy as jnp
from jax import lax
from jax.sharding import PartitionSpec as P

HEADS = 16
KVH = 4
HDIM = 128
BLK = 128
epsilon = 1e-05


def with_halo(cells, sides, width):
    for axis, dim in sides:
        count = lax.axis_size(axis)
        ends = count - 1
        head = lax.slice_in_dim(cells, 0, width, axis=dim)
        tail = lax.slice_in_dim(cells, cells.shape[dim] - width, cells.shape[dim], axis=dim)
        cells = jnp.concatenate(
            [
                lax.ppermute(tail, axis, [(i, (i + 1) % count) for i in range(ends)]),
                cells,
                lax.ppermute(head, axis, [((i + 1) % count, i) for i in range(ends)]),
            ],
            axis=dim,
        )
    return cells


def spread_2(value, axis, source):
    kept = jnp.where(lax.axis_index(axis) == source, value, 0).astype(value.dtype)
    return lax.psum(kept, axis)


def normalize(values):
    widened = values.astype(jnp.float32)
    inv_rms = lax.rsqrt(jnp.mean(widened * widened, axis=1, keepdims=True) + epsilon)
    return (widened * inv_rms, inv_rms)


def split_heads(row_values, block_count):
    return row_values.reshape(block_count, BLK, KVH, HEADS // KVH, HDIM)


def body(hidden, w_query, w_keyval, w_out, global_blocks, cotangent):
    row_count = hidden.shape[0]
    per_device = row_count // BLK
    block_count = 2 * per_device
    kv_width = w_keyval.shape[1]
    half_width = kv_width // 2
    global_count = global_blocks.shape[0]
    devices = lax.axis_size("ctx")
    my_index = lax.axis_index("ctx")
    full_query, full_keyval, full_output = (
        lax.all_gather(w_query, "ctx", axis=0, tiled=True),
        lax.all_gather(w_keyval, "ctx", axis=0, tiled=True),
        lax.all_gather(w_out, "ctx", axis=0, tiled=True),
    )
    stacked = jnp.concatenate([hidden, hidden[::-1, ::-1]], axis=0)
    scaled, inv_rms = normalize(stacked)
    normed = scaled.astype(jnp.bfloat16)
    queries = jnp.dot(normed, full_query, preferred_element_type=jnp.float32).astype(jnp.bfloat16)
    keyvals = jnp.dot(normed, full_keyval, preferred_element_type=jnp.float32).astype(jnp.bfloat16)
    kv_blocks = keyvals.reshape(2, per_device, BLK, kv_width)
    border = jnp.concatenate([kv_blocks[1, -1], kv_blocks[0, -1]], axis=0)
    padded = with_halo(border, (("ctx", 0),), BLK)
    neighbors = jnp.stack([padded[:BLK], padded[3 * BLK :]])
    extended = jnp.concatenate([neighbors[:, None], kv_blocks], axis=1)
    slot_index = global_blocks % per_device
    plain_owner = global_blocks // per_device
    owners = jnp.stack([plain_owner, devices - 1 - plain_owner])
    pieces = jnp.take(kv_blocks, slot_index, axis=1)
    collected = []
    for branch in range(2):
        for position in range(global_count):
            collected.append(spread_2(pieces[branch, position], "ctx", owners[branch, position]))
    global_keys = jnp.stack(collected).reshape(2, global_count, BLK, kv_width)
    paired = jnp.concatenate([extended[:, :-1], extended[:, 1:]], axis=2)
    spread = global_keys.reshape(2, 1, global_count * BLK, kv_width)
    key_sets = jnp.concatenate([paired, spread], axis=2).reshape(block_count, -1, kv_width)
    key_count = key_sets.shape[1]
    keys_only = key_sets[:, :, :half_width].reshape(block_count, key_count, KVH, HDIM)
    values_only = key_sets[:, :, half_width:].reshape(block_count, key_count, KVH, HDIM)
    first_ids = jnp.stack([my_index * per_device, (devices - 1 - my_index) * per_device])
    block_ids = (first_ids[:, None] + jnp.arange(per_device)[None, :]).reshape(block_count)
    global_flags = (global_blocks[None, :] != block_ids[:, None]) & (
        global_blocks[None, :] != block_ids[:, None] - 1
    )
    key_flags = jnp.concatenate(
        [(block_ids >= 1)[:, None], (block_ids >= 0)[:, None], global_flags], axis=1
    )
    validity = jnp.repeat(key_flags, BLK, axis=1)[:, None, None, None, :]
    query_heads = split_heads(queries, block_count)
    scores = jnp.einsum(
        "bqgrd,bkgd->bgrqk", query_heads, keys_only, preferred_element_type=jnp.float32
    ) * HDIM ** (-0.5)
    scores = jnp.where(validity, scores, -jnp.inf)
    exponent = jnp.exp(scores - jnp.max(scores, axis=-1, keepdims=True))
    prob_full = exponent / jnp.sum(exponent, axis=-1, keepdims=True)
    prob_half = prob_full.astype(jnp.bfloat16)
    attended = jnp.einsum(
        "bgrqk,bkgd->bqgrd", prob_half, values_only, preferred_element_type=jnp.float32
    )
    attended = attended.astype(jnp.bfloat16).reshape(2 * row_count, -1)
    outputs = jnp.dot(attended, full_output, preferred_element_type=jnp.float32)
    combined = (outputs[:row_count] + outputs[row_count:][::-1]).astype(jnp.bfloat16)
    grad_rows = jnp.concatenate([cotangent, cotangent[::-1]], axis=0)
    grad_att = jnp.dot(grad_rows, full_output.T, preferred_element_type=jnp.float32).astype(
        jnp.bfloat16
    )
    upstream = split_heads(grad_att, block_count)
    grad_prob = jnp.einsum(
        "bqgrd,bkgd->bgrqk", upstream, values_only, preferred_element_type=jnp.float32
    )
    center = jnp.sum(prob_full * grad_prob, axis=-1, keepdims=True)
    grad_score = (prob_full * (grad_prob - center) * HDIM ** (-0.5)).astype(jnp.bfloat16)
    grad_query = jnp.einsum(
        "bgrqk,bkgd->bqgrd", grad_score, keys_only, preferred_element_type=jnp.float32
    )
    grad_query = grad_query.astype(jnp.bfloat16).reshape(2 * row_count, -1)
    grad_keys = jnp.einsum(
        "bgrqk,bqgrd->bkgd", grad_score, query_heads, preferred_element_type=jnp.float32
    ).reshape(block_count, key_count, half_width)
    grad_values = jnp.einsum(
        "bgrqk,bqgrd->bkgd", prob_half, upstream, preferred_element_type=jnp.float32
    ).reshape(block_count, key_count, half_width)
    key_terms = jnp.concatenate([grad_keys, grad_values], axis=-1).reshape(
        2, per_device, 2 + global_count, BLK, kv_width
    )
    ext_grad = jnp.pad(key_terms[:, :, 0], ((0, 0), (0, 1), (0, 0), (0, 0))) + jnp.pad(
        key_terms[:, :, 1], ((0, 0), (1, 0), (0, 0), (0, 0))
    )
    outgoing = jnp.concatenate([ext_grad[0, 0], ext_grad[1, 0]], axis=0)
    returned = with_halo(outgoing.astype(jnp.bfloat16), (("ctx", 0),), BLK).astype(outgoing.dtype)
    own_grads = ext_grad[:, 1:]
    own_grads = own_grads.at[0, -1].add(returned[3 * BLK :])
    own_grads = own_grads.at[1, -1].add(returned[:BLK])
    totals = lax.psum(jnp.sum(key_terms[:, :, 2:], axis=1), "ctx")
    hot_table = (
        (jnp.arange(per_device)[None, None, :] == slot_index[None, :, None])
        & (owners[:, :, None] == my_index)
    ).astype(jnp.float32)
    own_grads = own_grads + jnp.sum(hot_table[:, :, :, None, None] * totals[:, :, None], axis=1)
    key_grads = own_grads.reshape(2 * row_count, kv_width).astype(jnp.bfloat16)
    grad_norm = jnp.dot(grad_query, full_query.T, preferred_element_type=jnp.float32)
    grad_norm = grad_norm + jnp.dot(key_grads, full_keyval.T, preferred_element_type=jnp.float32)
    grad_in = inv_rms * (grad_norm - scaled * jnp.mean(grad_norm * scaled, axis=1, keepdims=True))
    input_grad = (grad_in[:row_count] + grad_in[row_count:][::-1, ::-1]).astype(jnp.bfloat16)
    return (combined, input_grad)


def solution(mesh):
    return jax.shard_map(
        body,
        mesh=mesh,
        in_specs=(
            P(("groups", "ctx"), None),
            P("ctx", None),
            P("ctx", None),
            P("ctx", None),
            P("groups"),
            P(("groups", "ctx"), None),
        ),
        out_specs=(P(("groups", "ctx"), None), P(("groups", "ctx"), None)),
        check_vma=False,
    )
```

profile of v0, /device:TPU:0, one launch (start us, length us, event | category | flops | bytes accessed | tf_op | source)
XLA Modules:
  0.0 514.8 jit_solution(2713949893909427027)
XLA Ops:
  7.9 7.0 %rev.12 = bf16[128,2048]{1,0:T(8,128)(2,1)S(1)} reverse(bf16[128,2048]{1,0:T(8,128)(2,1)} %param.10), dimensions={0,1} | reverse | bytes 1048576 | tf_op jit(solution)/shard_map/rev | solution.py:59
  21.7 41.7 %all-gather.4.cloned.1.call-done = bf16[2048,1024]{1,0:T(8,128)(2,1)} async-done(((bf16[128,1024]{1,0:T(8,128)(2,1)}), bf16[2048,1024]{1,0:T(8,128)(2,1)}) %all-gather.4.cloned.1.call-update) | async-done | bytes 4194320 | tf_op jit(solution)/shard_map/all_gather | solution.py:56
  63.5 3.6 convolution_convert_fusion.2
  71.1 3.0 collective-permute-start
  74.2 5.2 %rev.14 = bf16[128,2048]{1,0:T(8,128)(2,1)} reverse(bf16[128,2048]{1,0:T(8,128)(2,1)S(1)} %copy-done.12), dimensions={0} | reverse | bytes 1048576 | tf_op jit(solution)/shard_map/rev | solution.py:107
  81.5 79.1 %all-reduce.8.cloned.1.call-done = (bf16[1,128,1024]{2,1,0:T(8,128)(2,1)}, bf16[1,128,1024]{2,1,0:T(8,128)(2,1)}, bf16[1,128,1024]{2,1,0:T(8,128)(2,1)}, bf16[1,128,1024]{2,1,0:T(8,128)(2,1)}) async-done(((bf16[1,128,1024]{2,1,0:T(8,128)(2,1)}, bf16[1,128,1024]{2,1,0:T(8,128)(2,1)}, bf16[1,128,1024]{2,1,0:T(8,128)(2,1)}, bf16[1,128,1024]{2,1,0:T(8,128)(2,1)}), (bf16[1,128,1024]{2,1,0:T(8,128)(2,1)}, ...) | async-done | bytes 1048592 | tf_op jit(solution)/shard_map/psum | solution.py:32
  165.1 72.0 %all-gather.6.cloned.1.call-done = bf16[2048,2048]{1,0:T(8,128)(2,1)} async-done(((bf16[128,2048]{1,0:T(8,128)(2,1)}), bf16[2048,2048]{1,0:T(8,128)(2,1)}) %all-gather.6.cloned.1.call-update) | async-done | bytes 8388624 | tf_op jit(solution)/shard_map/all_gather | solution.py:55
  237.2 5.8 %convolution_convert_fusion.1 = bf16[256,2048]{1,0:T(8,128)(2,1)S(1)} fusion(bf16[2048,2048]{1,0:T(8,128)(2,1)} %all-gather.6.cloned.1.call-done, f32[256]{0:T(256)S(1)} %add_rsqrt_fusion, bf16[128,2048]{1,0:T(8,128)(2,1)S(1)} %rev.12, bf16[128,2048]{1,0:T(8,128)(2,1)S(1)} %copy-done.2), kind=kOutput, calls=%fused_computation.31 | convolution fusion | flops 2151153664 | bytes 10486784 | tf_op jit(solution)/shard_map/dot_general | solution.py:62
  245.4 67.0 %all-gather.8.cloned.1.call-done = bf16[2048,2048]{1,0:T(8,128)(2,1)} async-done(((bf16[128,2048]{1,0:T(8,128)(2,1)}), bf16[2048,2048]{1,0:T(8,128)(2,1)}) %all-gather.8.cloned.1.call-update) | async-done | bytes 8388624 | tf_op jit(solution)/shard_map/all_gather | solution.py:57
  312.3 6.1 %convolution_convert_fusion = bf16[256,2048]{1,0:T(8,128)(2,1)S(1)} fusion(bf16[2048,2048]{1,0:T(8,128)(2,1)} %all-gather.8.cloned.1.call-done, bf16[128,2048]{1,0:T(8,128)(2,1)} %rev.14, bf16[128,2048]{1,0:T(8,128)(2,1)} %param.15), kind=kOutput, calls=%fused_computation.30 | convolution fusion | flops 2150105088 | bytes 10485760 | tf_op jit(solution)/shard_map/dot_general | solution.py:108
  320.4 4.5 fusion.69
  324.9 7.5 %fusion.67 = (f32[2,4,4,128]{3,2,1,0:T(4,128)S(1)}, f32[2,4,4,128,512]{3,4,2,1,0:T(8,128)}) fusion(pred[2,512]{1,0:T(4,128)(4,1)S(1)} %bitcast.176, bf16[2,512,4,128,1]{1,3,4,2,0:T(8,128)(2,1)} %bitcast.170, bf16[2,128,4,4,128]{1,4,3,2,0:T(8,128)(2,1)S(1)} %copy-done.10), kind=kOutput, calls=%fused_computation.108 | convolution fusion | flops 545260032 | bytes 10503168 | tf_op jit(solution)/shard_map/sub | solution.py:98
  332.4 5.3 %fusion.37 = bf16[2,128,4,4,128]{1,4,3,2,0:T(8,128)(2,1)} fusion(bf16[2,512,4,128,1]{1,3,4,2,0:T(8,128)(2,1)S(1)} %bitcast.166, f32[2,4,4,128,512]{3,4,2,1,0:T(8,128)} %get-tuple-element.49, f32[2,4,4,128]{3,2,1,0:T(4,128)S(1)} %get-tuple-element.48), kind=kOutput, calls=%fused_computation.50 | convolution fusion | flops 541589504 | bytes 10502144 | tf_op jit(solution)/shard_map/bgrqk,bkgd->bqgrd/dot_general | solution.py:101
  340.1 14.6 %fusion.36 = bf16[2,128,4,4,128]{1,4,3,2,0:T(8,128)(2,1)} fusion(bf16[2,512,4,128,1]{1,3,4,2,0:T(8,128)(2,1)} %bitcast.171, f32[2,4,512,128,4]{3,2,4,1,0:T(8,128)} %fusion.69, f32[2,4,4,128,512]{3,4,2,1,0:T(8,128)} %get-tuple-element.49, f32[2,4,4,128]{3,2,1,0:T(4,128)S(1)} %get-tuple-element.48), kind=kOutput, calls=%fused_computation.49 | convolution fusion | flops 552079872 | bytes 18890752 | tf_op jit(solution)/shard_map/bgrqk,bkgd->bqgrd/dot_general | solution.py:117
  354.6 13.4 %fusion.31 = f32[2,512,4,128]{1,3,2,0:T(8,128)} fusion(bf16[2,128,4,4,128]{1,4,3,2,0:T(8,128)(2,1)S(1)} %copy-done.11, f32[2,4,512,128,4]{3,2,4,1,0:T(8,128)} %fusion.69, f32[2,4,4,128,512]{3,4,2,1,0:T(8,128)} %get-tuple-element.49, f32[2,4,4,128]{3,2,1,0:T(4,128)S(1)} %get-tuple-element.48), kind=kOutput, calls=%fused_computation.46 | convolution fusion | flops 551555584 | bytes 19939328 | tf_op jit(solution)/shard_map/bgrqk,bqgrd->bkgd/dot_general | solution.py:121
  368.1 1.7 concatenate.59
  369.8 1.9 copy.39
  371.7 2.9 concatenate.58
  374.6 2.9 copy.38
  377.5 2.5 maximum_bitcast_fusion.2
  381.5 2.0 copy.29
  383.5 1.9 reshape.285
  385.4 1.9 copy.33
  391.1 3.7 collective-permute-start.2
  394.9 5.8 %fusion.68 = f32[256,2048]{1,0:T(8,128)S(1)} fusion(bf16[256,2048]{1,0:T(8,128)(2,1)S(1)} %copy-done.8, bf16[2048,2048]{1,0:T(8,128)(2,1)} %all-gather.8.cloned.1.call-done), kind=kOutput, calls=%fused_computation.109 | convolution fusion | flops 2147483648 | bytes 11534336 | tf_op jit(solution)/shard_map/dot_general | solution.py:105
  400.7 7.9 %fusion.70 = f32[256,2048]{1,0:T(8,128)} fusion(bf16[256,2048]{1,0:T(8,128)(2,1)S(1)} %copy-done.9, bf16[2048,2048]{1,0:T(8,128)(2,1)} %all-gather.6.cloned.1.call-done), kind=kOutput, calls=%fused_computation.111 | convolution fusion | flops 2147483648 | bytes 11534336 | tf_op jit(solution)/shard_map/dot_general | solution.py:145
  409.7 6.8 %rev.13 = f32[128,2048]{1,0:T(8,128)S(1)} reverse(f32[128,2048]{1,0:T(8,128)} %slice.178), dimensions={0} | reverse | bytes 2097152 | tf_op jit(solution)/shard_map/rev | solution.py:106
  416.6 2.1 fusion.42
  421.1 71.3 %all-reduce.6.cloned.1.call-done = f32[2,2,128,1024]{3,2,0,1:T(8,128)} async-done(((f32[2,2,128,1024]{3,2,0,1:T(8,128)}), f32[2,2,128,1024]{3,2,0,1:T(8,128)}) %all-reduce.6.cloned.1.call-update) | async-done | bytes 2097168 | tf_op jit(solution)/shard_map/psum | solution.py:138
  492.4 2.2 multiply_reduce_fusion
  495.2 3.1 fusion.18
  499.8 7.5 %rev.15 = f32[128,2048]{1,0:T(8,128)S(1)} reverse(f32[128,2048]{1,0:T(8,128)} %slice.187), dimensions={0,1} | reverse | bytes 2097152 | tf_op jit(solution)/shard_map/rev | solution.py:148
  (86 shorter events, 33.9 us)
Async XLA Ops:
  7.2 56.3 %all-gather.4.cloned.1.call-start = ((), (), s32[]{:S(2)}) async-start(), calls=%async_computation | async-start | bytes 4456448 | tf_op jit(solution)/shard_map/all_gather | solution.py:56
  7.9 152.8 %all-reduce.8.cloned.1.call-start = ((), (), s32[]{:S(2)}) async-start(), calls=%async_computation.4 | async-start | bytes 2097152 | tf_op jit(solution)/shard_map/psum | solution.py:32
  14.9 222.2 %copy-start.4 = (bf16[128,2048]{1,0:T(8,128)(2,1)}, bf16[128,2048]{1,0:T(8,128)(2,1)S(1)}, u32[]{:S(2)}) copy-start(bf16[128,2048]{1,0:T(8,128)(2,1)S(1)} %rev.12) | copy-start | bytes 1572868
  21.7 47.9 %copy-start.13 = (s32[2]{0:T(128)S(1)}, s32[2]{0:T(128)}, u32[]{:S(2)}) copy-start(s32[2]{0:T(128)} %param.14) | copy-start | bytes 28
  21.7 52.5 %copy-start.12 = (bf16[128,2048]{1,0:T(8,128)(2,1)S(1)}, bf16[128,2048]{1,0:T(8,128)(2,1)}, u32[]{:S(2)}) copy-start(bf16[128,2048]{1,0:T(8,128)(2,1)} %param.15) | copy-start | bytes 1572868
  68.2 169.0 %all-gather.6.cloned.1.call-start = ((), (), s32[]{:S(2)}) async-start(), calls=%async_computation.1 | async-start | bytes 8912896 | tf_op jit(solution)/shard_map/all_gather | solution.py:55
  68.9 243.4 %all-gather.8.cloned.1.call-start = ((), (), s32[]{:S(2)}) async-start(), calls=%async_computation.2 | async-start | bytes 8912896 | tf_op jit(solution)/shard_map/all_gather | solution.py:57
  69.5 422.9 %all-reduce.6.cloned.1.call-start = ((), (), s32[]{:S(2)}) async-start(), calls=%async_computation.3 | async-start | bytes 4194304 | tf_op jit(solution)/shard_map/psum | solution.py:138
  69.8 10.7 %collective-permute-start.1 = (bf16[128,1024]{1,0:T(8,128)(2,1)S(1)}, bf16[128,1024]{1,0:T(8,128)(2,1)S(1)}, u32[]{:S(2)}, u32[]{:S(2)}) collective-permute-start(bf16[128,1024]{1,0:T(8,128)(2,1)S(1)} %get-tuple-element.43), channel_id=1, source_target_pairs={{1,0},{2,1},{3,2},{4,3},{5,4},{6,5},{7,6},{8,7},{9,8},{10,9},{11,1... | collective-permute-start | bytes 786440 | tf_op jit(solution)/shard_map/ppermute | solution.py:23
  71.1 9.4 %collective-permute-start = (bf16[128,1024]{1,0:T(8,128)(2,1)S(1)}, bf16[128,1024]{1,0:T(8,128)(2,1)S(1)}, u32[]{:S(2)}, u32[]{:S(2)}) collective-permute-start(bf16[128,1024]{1,0:T(8,128)(2,1)S(1)} %get-tuple-element.38), channel_id=1, source_target_pairs={{0,1},{1,2},{2,3},{3,4},{4,5},{5,6},{6,7},{7,8},{8,9},{9,10},{10,1... | collective-permute-start | bytes 786440 | tf_op jit(solution)/shard_map/ppermute | solution.py:21
  162.5 74.6 %copy-start.2 = (bf16[128,2048]{1,0:T(8,128)(2,1)S(1)}, bf16[128,2048]{1,0:T(8,128)(2,1)}, u32[]{:S(2)}) copy-start(bf16[128,2048]{1,0:T(8,128)(2,1)} %param.10) | copy-start | bytes 1572868
  320.4 4.5 copy-start.10
  332.4 6.1 %copy-start.14 = (f32[2,4,4,128,512]{3,4,2,1,0:T(8,128)S(1)}, f32[2,4,4,128,512]{3,4,2,1,0:T(8,128)}, u32[]{:S(2)}) copy-start(f32[2,4,4,128,512]{3,4,2,1,0:T(8,128)} %get-tuple-element.49) | copy-start | bytes 25165828
  340.1 14.6 %copy-start.11 = (bf16[2,128,4,4,128]{1,4,3,2,0:T(8,128)(2,1)S(1)}, bf16[2,128,4,4,128]{1,4,3,2,0:T(8,128)(2,1)}, u32[]{:S(2)}) copy-start(bf16[2,128,4,4,128]{1,4,3,2,0:T(8,128)(2,1)} %copy.34) | copy-start | bytes 3145732
  377.5 2.5 copy-start
  381.5 7.4 %copy-start.1 = (f32[2,1,128,1024]{3,2,1,0:T(8,128)S(1)}, f32[2,1,128,1024]{3,2,1,0:T(8,128)}, u32[]{:S(2)}) copy-start(f32[2,1,128,1024]{3,2,1,0:T(8,128)} %get-tuple-element.33) | copy-start | bytes 3145732
  388.9 5.9 %copy-start.8 = (bf16[256,2048]{1,0:T(8,128)(2,1)S(1)}, bf16[256,2048]{1,0:T(8,128)(2,1)}, u32[]{:S(2)}) copy-start(bf16[256,2048]{1,0:T(8,128)(2,1)} %reshape.285) | copy-start | bytes 3145732
  389.8 29.0 %collective-permute-start.3 = (bf16[128,1024]{1,0:T(8,128)(2,1)}, bf16[128,1024]{1,0:T(8,128)(2,1)}, u32[]{:S(2)}, u32[]{:S(2)}) collective-permute-start(bf16[128,1024]{1,0:T(8,128)(2,1)} %get-tuple-element.37), channel_id=1, source_target_pairs={{1,0},{2,1},{3,2},{4,3},{5,4},{6,5},{7,6},{8,7},{9,8},{10,9},{11,1... | collective-permute-start | bytes 786440 | tf_op jit(solution)/shard_map/ppermute | solution.py:23
  391.1 27.7 %collective-permute-start.2 = (bf16[128,1024]{1,0:T(8,128)(2,1)S(1)}, bf16[128,1024]{1,0:T(8,128)(2,1)}, u32[]{:S(2)}, u32[]{:S(2)}) collective-permute-start(bf16[128,1024]{1,0:T(8,128)(2,1)S(1)} %get-tuple-element.36), channel_id=1, source_target_pairs={{0,1},{1,2},{2,3},{3,4},{4,5},{5,6},{6,7},{7,8},{8,9},{9,10},{10,1... | collective-permute-start | bytes 786440 | tf_op jit(solution)/shard_map/ppermute | solution.py:21
  394.9 5.8 %copy-start.9 = (bf16[256,2048]{1,0:T(8,128)(2,1)S(1)}, bf16[256,2048]{1,0:T(8,128)(2,1)}, u32[]{:S(2)}) copy-start(bf16[256,2048]{1,0:T(8,128)(2,1)} %reshape.287) | copy-start | bytes 3145732
  400.7 7.9 %copy-start.7 = (f32[256,2048]{1,0:T(8,128)}, f32[256,2048]{1,0:T(8,128)S(1)}, u32[]{:S(2)}) copy-start(f32[256,2048]{1,0:T(8,128)S(1)} %fusion.68) | copy-start | bytes 6291460
  420.0 74.8 %copy-start.3 = (bf16[128,2048]{1,0:T(8,128)(2,1)S(1)}, bf16[128,2048]{1,0:T(8,128)(2,1)}, u32[]{:S(2)}) copy-start(bf16[128,2048]{1,0:T(8,128)(2,1)} %param.10) | copy-start | bytes 1572868
  420.0 74.8 %copy-start.5 = (bf16[128,2048]{1,0:T(8,128)(2,1)S(1)}, bf16[128,2048]{1,0:T(8,128)(2,1)}, u32[]{:S(2)}) copy-start(bf16[128,2048]{1,0:T(8,128)(2,1)} %copy-done.4) | copy-start | bytes 1572868
  492.4 2.8 copy-start.6
Sparse Core Ops, SparseCore 0:
  10.2 53.2 all-gather.3
  68.3 92.3 all-reduce.7
  162.8 74.2 all-gather.5
  239.2 73.1 all-gather.7
  395.0 97.3 all-reduce.5
where the time goes:
time: 517 us; the launch traced here: 515 us
  waiting for transfers between devices  333 us (64%)
  matrix products  79.2 us (15%)
  local copies, waits for them, and re-layouts  57.9 us (11%)
  other arithmetic  18.3 us (4%)
  between operations  16.8 us (3%)
  starting transfers between devices  9.53 us (2%)
    psum x1, waiting for transfers between devices, spread_2(): return lax.psum(kept, axis)  79.1 us
    all_gather x1, waiting for transfers between devices, body(): lax.all_gather(w_query, 'ctx', axis=0, tiled=True)  72 us
    psum x1, waiting for transfers between devices, body(): totals = lax.psum(jnp.sum(key_terms[:, :, 2:], axis=1), 'ctx')  71.3 us
    all_gather x1, waiting for transfers between devices, body(): lax.all_gather(w_out, 'ctx', axis=0, tiled=True)  67 us
    all_gather x1, waiting for transfers between devices, body(): lax.all_gather(w_keyval, 'ctx', axis=0, tiled=True)  41.7 us
    dot_general x1, matrix products, body(): jnp.einsum('bgrqk,bkgd->bqgrd', grad_score, keys_only, preferred_element_...  14.6 us
    dot_general x1, matrix products, body(): jnp.einsum('bgrqk,bqgrd->bkgd', grad_score, query_heads, preferred_elemen...  13.4 us
  transfers between devices with their start and end apart: 9, of which 5 were waited for; matrix products, arithmetic and copies ran while one was open for 11% of the time, Pallas kernels for 0%

commit v1 on v0

--- a/solution.py
+++ b/solution.py
@@ -135,7 +135,7 @@
     own_grads = ext_grad[:, 1:]
     own_grads = own_grads.at[0, -1].add(returned[3 * BLK :])
     own_grads = own_grads.at[1, -1].add(returned[:BLK])
-    totals = lax.psum(jnp.sum(key_terms[:, :, 2:], axis=1), "ctx")
+    totals = jnp.sum(lax.all_gather(jnp.sum(key_terms[:, :, 2:], axis=1), "ctx"), axis=0)
     hot_table = (
         (jnp.arange(per_device)[None, None, :] == slot_index[None, :, None])
         & (owners[:, :, None] == my_index)

time: 517 us -> 576 us (1.11)
  waiting for transfers between devices: 333 us -> 364 us
  local copies, waits for them, and re-layouts: 57.9 us -> 67.7 us
  other arithmetic: 18.3 us -> 27.7 us
  matrix products: 79.2 us -> 86.8 us
    all_gather x0 -> x1, waiting for transfers between devices: none -> 104 us  [body(): lax.all_gather(jnp.sum(key_terms[:, :, 2:], axis=1), 'ctx')]
    psum x1 -> x0, waiting for transfers between devices: 71.3 us -> none  [body(): totals = lax.psum(jnp.sum(key_terms[:, :, 2:], axis=1), 'ctx')]
    reduce_sum x1, other arithmetic: 1.5 us -> 12.1 us  [body(): jnp.sum(lax.all_gather(jnp.sum(key_terms[:, :, 2:], axis=1), 'ctx'), axis=0)]
  transfers between devices with their start and end apart: 9 -> 9, of which waited for: 5 -> 5; matrix products, arithmetic and copies ran while one was open for 11% -> 16% of each run, Pallas kernels for 0% -> 0%
where the time goes in v1:
time: 576 us; the launch traced here: 572 us
  waiting for transfers between devices  364 us (63%)
  matrix products  86.8 us (15%)
  local copies, waits for them, and re-layouts  67.7 us (12%)
  other arithmetic  27.7 us (5%)
  between operations  16.7 us (3%)
  starting transfers between devices  9.34 us (2%)
    all_gather x1, waiting for transfers between devices, body(): lax.all_gather(jnp.sum(key_terms[:, :, 2:], axis=1), 'ctx')  104 us
    psum x1, waiting for transfers between devices, spread_2(): return lax.psum(kept, axis)  79.1 us
    all_gather x1, waiting for transfers between devices, body(): lax.all_gather(w_query, 'ctx', axis=0, tiled=True)  72 us
    all_gather x1, waiting for transfers between devices, body(): lax.all_gather(w_out, 'ctx', axis=0, tiled=True)  64.9 us
    all_gather x1, waiting for transfers between devices, body(): lax.all_gather(w_keyval, 'ctx', axis=0, tiled=True)  42 us
    dot_general x1, matrix products, body(): jnp.einsum('bgrqk,bkgd->bqgrd', grad_score, keys_only, preferred_element_...  15.1 us
    dot_general x1, matrix products, body(): jnp.einsum('bgrqk,bqgrd->bkgd', grad_score, query_heads, preferred_elemen...  14.8 us
    reduce_sum x1, other arithmetic, body(): jnp.sum(lax.all_gather(jnp.sum(key_terms[:, :, 2:], axis=1), 'ctx'), axis=0)  12.1 us
  transfers between devices with their start and end apart: 9, of which 5 were waited for; matrix products, arithmetic and copies ran while one was open for 16% of the time, Pallas kernels for 0%

profile of v1, /device:TPU:0, one launch (start us, length us, event | category | flops | bytes accessed | tf_op | source)
XLA Modules:
  0.0 572.0 jit_solution(10216869749436170754)
XLA Ops:
  7.9 7.0 %rev.12 = bf16[128,2048]{1,0:T(8,128)(2,1)S(1)} reverse(bf16[128,2048]{1,0:T(8,128)(2,1)} %param.10), dimensions={0,1} | reverse | bytes 1048576 | tf_op jit(solution)/shard_map/rev | solution.py:59
  21.5 42.0 %all-gather.6.cloned.1.call-done = bf16[2048,1024]{1,0:T(8,128)(2,1)} async-done(((bf16[128,1024]{1,0:T(8,128)(2,1)}), bf16[2048,1024]{1,0:T(8,128)(2,1)}) %all-gather.6.cloned.1.call-update) | async-done | bytes 4194320 | tf_op jit(solution)/shard_map/all_gather | solution.py:56
  63.5 3.6 convolution_convert_fusion.2
  71.0 3.0 collective-permute-start
  74.2 5.2 rev.14
  81.5 79.1 %all-reduce.5.cloned.1.call-done = (bf16[1,128,1024]{2,1,0:T(8,128)(2,1)}, bf16[1,128,1024]{2,1,0:T(8,128)(2,1)}, bf16[1,128,1024]{2,1,0:T(8,128)(2,1)}, bf16[1,128,1024]{2,1,0:T(8,128)(2,1)}) async-done(((bf16[1,128,1024]{2,1,0:T(8,128)(2,1)}, bf16[1,128,1024]{2,1,0:T(8,128)(2,1)}, bf16[1,128,1024]{2,1,0:T(8,128)(2,1)}, bf16[1,128,1024]{2,1,0:T(8,128)(2,1)}), (bf16[1,128,1024]{2,1,0:T(8,128)(2,1)}, ...) | async-done | bytes 1048592 | tf_op jit(solution)/shard_map/psum | solution.py:32
  165.1 72.0 %all-gather.8.cloned.1.call-done = bf16[2048,2048]{1,0:T(8,128)(2,1)} async-done(((bf16[128,2048]{1,0:T(8,128)(2,1)}), bf16[2048,2048]{1,0:T(8,128)(2,1)}) %all-gather.8.cloned.1.call-update) | async-done | bytes 8388624 | tf_op jit(solution)/shard_map/all_gather | solution.py:55
  237.1 6.7 %convolution_convert_fusion.1 = bf16[256,2048]{1,0:T(8,128)(2,1)} fusion(bf16[2048,2048]{1,0:T(8,128)(2,1)} %all-gather.8.cloned.1.call-done, f32[256]{0:T(256)S(1)} %add_rsqrt_fusion, bf16[128,2048]{1,0:T(8,128)(2,1)S(1)} %rev.12, bf16[128,2048]{1,0:T(8,128)(2,1)S(1)} %copy-done), kind=kOutput, calls=%fused_computation.31 | convolution fusion | flops 2151153664 | bytes 10486784 | tf_op jit(solution)/shard_map/dot_general | solution.py:62
  247.3 64.9 %all-gather.10.cloned.1.call-done = bf16[2048,2048]{1,0:T(8,128)(2,1)} async-done(((bf16[128,2048]{1,0:T(8,128)(2,1)}), bf16[2048,2048]{1,0:T(8,128)(2,1)}) %all-gather.10.cloned.1.call-update) | async-done | bytes 8388624 | tf_op jit(solution)/shard_map/all_gather | solution.py:57
  312.3 6.1 %convolution_convert_fusion = bf16[256,2048]{1,0:T(8,128)(2,1)S(1)} fusion(bf16[2048,2048]{1,0:T(8,128)(2,1)} %all-gather.10.cloned.1.call-done, bf16[128,2048]{1,0:T(8,128)(2,1)} %rev.14, bf16[128,2048]{1,0:T(8,128)(2,1)} %param.15), kind=kOutput, calls=%fused_computation.30 | convolution fusion | flops 2150105088 | bytes 10485760 | tf_op jit(solution)/shard_map/dot_general | solution.py:108
  321.9 4.5 fusion.68
  326.4 7.8 %fusion.66 = (f32[2,4,4,128]{3,2,1,0:T(4,128)S(1)}, f32[2,4,4,128,512]{3,4,2,1,0:T(8,128)}) fusion(pred[2,512]{1,0:T(4,128)(4,1)S(1)} %bitcast.176, bf16[2,512,4,128,1]{1,3,4,2,0:T(8,128)(2,1)} %bitcast.170, bf16[2,128,4,4,128]{1,4,3,2,0:T(8,128)(2,1)} %copy.54), kind=kOutput, calls=%fused_computation.107 | convolution fusion | flops 545260032 | bytes 10503168 | tf_op jit(solution)/shard_map/sub | solution.py:98
  334.2 6.2 %fusion.27 = f32[2,512,4,128]{1,3,2,0:T(8,128)} fusion(bf16[2,128,4,4,128]{1,4,3,2,0:T(8,128)(2,1)S(1)} %copy.56, f32[2,4,4,128,512]{3,4,2,1,0:T(8,128)} %get-tuple-element.49, f32[2,4,4,128]{3,2,1,0:T(4,128)S(1)} %get-tuple-element.48), kind=kOutput, calls=%fused_computation.44 | convolution fusion | flops 541065216 | bytes 11550720 | tf_op jit(solution)/shard_map/bgrqk,bqgrd->bkgd/dot_general | solution.py:124
  340.4 2.9 concatenate.59
  345.2 14.8 %fusion.30 = f32[2,512,4,128]{1,3,2,0:T(8,128)} fusion(bf16[2,128,4,4,128]{1,4,3,2,0:T(8,128)(2,1)} %copy.54, f32[2,4,512,128,4]{3,2,4,1,0:T(8,128)} %fusion.68, f32[2,4,4,128,512]{3,4,2,1,0:T(8,128)} %get-tuple-element.49, f32[2,4,4,128]{3,2,1,0:T(4,128)S(1)} %get-tuple-element.48), kind=kOutput, calls=%fused_computation.45 | convolution fusion | flops 551555584 | bytes 19939328 | tf_op jit(solution)/shard_map/bgrqk,bqgrd->bkgd/dot_general | solution.py:121
  360.0 2.9 concatenate.58
  362.9 2.9 copy.58
  365.8 2.7 pad_maximum_fusion
  368.7 5.5 fusion.36
  374.1 2.7 copy.49
  376.8 2.6 reshape.287
  379.4 6.3 %fusion.67 = f32[256,2048]{1,0:T(8,128)S(1)} fusion(bf16[256,2048]{1,0:T(8,128)(2,1)} %reshape.287, bf16[2048,2048]{1,0:T(8,128)(2,1)} %all-gather.10.cloned.1.call-done), kind=kOutput, calls=%fused_computation.108 | convolution fusion | flops 2147483648 | bytes 11534336 | tf_op jit(solution)/shard_map/dot_general | solution.py:105
  388.1 8.9 %rev.13 = f32[128,2048]{1,0:T(8,128)} reverse(f32[128,2048]{1,0:T(8,128)} %slice.178), dimensions={0} | reverse | bytes 2097152 | tf_op jit(solution)/shard_map/rev | solution.py:106
  397.0 15.1 %fusion.35 = bf16[2,128,4,4,128]{1,4,3,2,0:T(8,128)(2,1)} fusion(bf16[2,512,4,128,1]{1,3,4,2,0:T(8,128)(2,1)} %bitcast.171, f32[2,4,512,128,4]{3,2,4,1,0:T(8,128)} %fusion.68, f32[2,4,4,128,512]{3,4,2,1,0:T(8,128)} %get-tuple-element.49, f32[2,4,4,128]{3,2,1,0:T(4,128)S(1)} %get-tuple-element.48), kind=kOutput, calls=%fused_computation.48 | convolution fusion | flops 552079872 | bytes 18890752 | tf_op jit(solution)/shard_map/bgrqk,bkgd->bqgrd/dot_general | solution.py:117
  412.1 2.6 copy.53
  414.8 2.6 reshape.289
  420.4 3.5 collective-permute-start.2
  423.9 7.1 %fusion.69 = f32[256,2048]{1,0:T(8,128)} fusion(bf16[256,2048]{1,0:T(8,128)(2,1)S(1)} %copy-done.6, bf16[2048,2048]{1,0:T(8,128)(2,1)} %all-gather.8.cloned.1.call-done), kind=kOutput, calls=%fused_computation.110 | convolution fusion | flops 2147483648 | bytes 11534336 | tf_op jit(solution)/shard_map/dot_general | solution.py:145
  434.0 103.9 %all-gather.12.cloned.1.call-done = f32[32,1,2,128,1024]{4,3,0,2,1:T(8,128)} async-done(((f32[2,1,2,128,1024]{4,3,0,2,1:T(8,128)}), f32[32,1,2,128,1024]{4,3,0,2,1:T(8,128)}) %all-gather.12.cloned.1.call-update) | async-done | bytes 33554448 | tf_op jit(solution)/shard_map/all_gather | solution.py:138
  537.8 12.1 %reduce_sum.63 = f32[2,2,128,1024]{3,2,0,1:T(8,128)S(1)} reduce(f32[16,2,2,128,1024]{4,3,1,0,2:T(8,128)} %bitcast.163, f32[]{:T(128)} %constant.114.clone.1), dimensions={0}, to_apply=%region_8.9 | reduce | flops 7864320 | bytes 35651588 | tf_op jit(solution)/shard_map/reduce_sum | solution.py:138
  552.5 3.1 fusion.18
  557.1 7.5 %rev.15 = f32[128,2048]{1,0:T(8,128)S(1)} reverse(f32[128,2048]{1,0:T(8,128)} %slice.187), dimensions={0,1} | reverse | bytes 2097152 | tf_op jit(solution)/shard_map/rev | solution.py:148
  (75 shorter events, 37.4 us)
Async XLA Ops:
  7.2 56.3 %all-gather.6.cloned.1.call-start = ((), (), s32[]{:S(2)}) async-start(), calls=%async_computation | async-start | bytes 4456448 | tf_op jit(solution)/shard_map/all_gather | solution.py:56
  7.9 152.7 %all-reduce.5.cloned.1.call-start = ((), (), s32[]{:S(2)}) async-start(), calls=%async_computation.4 | async-start | bytes 2097152 | tf_op jit(solution)/shard_map/psum | solution.py:32
  21.5 48.2 %copy-start.8 = (s32[2]{0:T(128)S(1)}, s32[2]{0:T(128)}, u32[]{:S(2)}) copy-start(s32[2]{0:T(128)} %param.14) | copy-start | bytes 28
  21.5 52.7 %copy-start.7 = (bf16[128,2048]{1,0:T(8,128)(2,1)S(1)}, bf16[128,2048]{1,0:T(8,128)(2,1)}, u32[]{:S(2)}) copy-start(bf16[128,2048]{1,0:T(8,128)(2,1)} %param.15) | copy-start | bytes 1572868
  68.2 168.9 %all-gather.8.cloned.1.call-start = ((), (), s32[]{:S(2)}) async-start(), calls=%async_computation.1 | async-start | bytes 8912896 | tf_op jit(solution)/shard_map/all_gather | solution.py:55
  68.9 243.4 %all-gather.10.cloned.1.call-start = ((), (), s32[]{:S(2)}) async-start(), calls=%async_computation.2 | async-start | bytes 8912896 | tf_op jit(solution)/shard_map/all_gather | solution.py:57
  69.5 468.3 %all-gather.12.cloned.1.call-start = ((), (), s32[]{:S(2)}) async-start(), calls=%async_computation.3 | async-start | bytes 35651584 | tf_op jit(solution)/shard_map/all_gather | solution.py:138
  69.7 10.7 %collective-permute-start.1 = (bf16[128,1024]{1,0:T(8,128)(2,1)S(1)}, bf16[128,1024]{1,0:T(8,128)(2,1)S(1)}, u32[]{:S(2)}, u32[]{:S(2)}) collective-permute-start(bf16[128,1024]{1,0:T(8,128)(2,1)S(1)} %get-tuple-element.43), channel_id=1, source_target_pairs={{1,0},{2,1},{3,2},{4,3},{5,4},{6,5},{7,6},{8,7},{9,8},{10,9},{11,1... | collective-permute-start | bytes 786440 | tf_op jit(solution)/shard_map/ppermute | solution.py:23
  71.0 9.4 %collective-permute-start = (bf16[128,1024]{1,0:T(8,128)(2,1)S(1)}, bf16[128,1024]{1,0:T(8,128)(2,1)S(1)}, u32[]{:S(2)}, u32[]{:S(2)}) collective-permute-start(bf16[128,1024]{1,0:T(8,128)(2,1)S(1)} %get-tuple-element.38), channel_id=1, source_target_pairs={{0,1},{1,2},{2,3},{3,4},{4,5},{5,6},{6,7},{7,8},{8,9},{9,10},{10,1... | collective-permute-start | bytes 786440 | tf_op jit(solution)/shard_map/ppermute | solution.py:21
  162.4 74.6 %copy-start = (bf16[128,2048]{1,0:T(8,128)(2,1)S(1)}, bf16[128,2048]{1,0:T(8,128)(2,1)}, u32[]{:S(2)}) copy-start(bf16[128,2048]{1,0:T(8,128)(2,1)} %param.10) | copy-start | bytes 1572868
  165.1 156.7 %copy-start.2 = (bf16[2,512,512]{1,2,0:T(8,128)(2,1)}, bf16[2,512,512]{1,2,0:T(8,128)(2,1)S(1)}, u32[]{:S(2)}) copy-start(bf16[2,512,512]{1,2,0:T(8,128)(2,1)S(1)} %get-tuple-element.35) | copy-start | bytes 3145732
  385.7 1.4 copy-start.4
  417.4 6.6 %copy-start.6 = (bf16[256,2048]{1,0:T(8,128)(2,1)S(1)}, bf16[256,2048]{1,0:T(8,128)(2,1)}, u32[]{:S(2)}) copy-start(bf16[256,2048]{1,0:T(8,128)(2,1)} %reshape.289) | copy-start | bytes 3145732
  419.1 12.9 %collective-permute-start.3 = (bf16[128,1024]{1,0:T(8,128)(2,1)S(1)}, bf16[128,1024]{1,0:T(8,128)(2,1)S(1)}, u32[]{:S(2)}, u32[]{:S(2)}) collective-permute-start(bf16[128,1024]{1,0:T(8,128)(2,1)S(1)} %get-tuple-element.37), channel_id=1, source_target_pairs={{1,0},{2,1},{3,2},{4,3},{5,4},{6,5},{7,6},{8,7},{9,8},{10,9},{11,1... | collective-permute-start | bytes 786440 | tf_op jit(solution)/shard_map/ppermute | solution.py:23
  420.4 10.6 %copy-start.3 = (f32[128,2048]{1,0:T(8,128)S(1)}, f32[128,2048]{1,0:T(8,128)}, u32[]{:S(2)}) copy-start(f32[128,2048]{1,0:T(8,128)} %rev.13) | copy-start | bytes 3145732
  420.4 10.6 %copy-start.5 = (f32[256,2048]{1,0:T(8,128)S(1)}, f32[256,2048]{1,0:T(8,128)}, u32[]{:S(2)}) copy-start(f32[256,2048]{1,0:T(8,128)} %copy-done.4) | copy-start | bytes 6291460
  420.4 11.6 %collective-permute-start.2 = (bf16[128,1024]{1,0:T(8,128)(2,1)S(1)}, bf16[128,1024]{1,0:T(8,128)(2,1)S(1)}, u32[]{:S(2)}, u32[]{:S(2)}) collective-permute-start(bf16[128,1024]{1,0:T(8,128)(2,1)S(1)} %get-tuple-element.36), channel_id=1, source_target_pairs={{0,1},{1,2},{2,3},{3,4},{4,5},{5,6},{6,7},{7,8},{8,9},{9,10},{10,1... | collective-permute-start | bytes 786440 | tf_op jit(solution)/shard_map/ppermute | solution.py:21
  550.0 2.5 copy-start.1
Sparse Core Ops, SparseCore 0:
  10.2 53.2 all-gather.5
  68.3 92.2 all-reduce.4
  162.8 74.2 all-gather.7
  239.1 73.1 all-gather.9
  368.7 169.1 all-gather.11
